TPU v7x, 32 devices: a whole 2x2x4 slice. The times are simulated.
32 devices in a mesh: expert: 8 (over y, x, core), tensor: 4 (over z).
Axes of the slice: x: 2, y: 2, z: 4, core: 2. Of those that a mesh axis runs over, the one named last changes fastest.
Arguments:
- tokens: bfloat16 [8192, 1024], P('expert'), may hold values from -6 to 6
- cotangent: bfloat16 [8192, 1024], P('expert'), may hold values from -6 to 6
- routes: int32 [8192], P('expert'), may hold values from 0 to 15, as said below
- slot_index: int32 [8192], P('expert'), may hold values from 0 to 128, as said below
- first_gain: float32 [1024], replicated, may hold values from 0.1 to 1.9
- first_shift: float32 [1024], replicated, may hold values from -1.25 to 1.25
- project_in: bfloat16 [1024, 3, 1024], P(None, None, 'tensor'), may hold values from -0.25 to 0.25
- project_out: bfloat16 [1024, 1024], P('tensor'), may hold values from -1.5 to 1.5
- second_gain: float32 [1024], replicated, may hold values from 0.1 to 1.9
- second_shift: float32 [1024], replicated, may hold values from -1.25 to 1.25
- router_weight: bfloat16 [1024, 16], replicated, may hold values from -0.09375 to 0.09375
- mixing_weight: bfloat16 [1024, 2], replicated, may hold values from -0.1875 to 0.1875
- dense_up: bfloat16 [1024, 4096], P(None, 'tensor'), may hold values from -0.1875 to 0.1875
- dense_down: bfloat16 [4096, 1024], P('tensor'), may hold values from -0.1875 to 0.1875
- expert_up: bfloat16 [16, 1024, 4096], P('expert', None, 'tensor'), may hold values from -0.375 to 0.375
- expert_down: bfloat16 [16, 4096, 1024], P('expert', 'tensor'), may hold values from -3 to 3
Outputs:
- layer_out: bfloat16 [8192, 1024], P('expert')
- input_grad: bfloat16 [8192, 1024], P('expert')
- first_gain_grad: float32 [1024], replicated
- first_shift_grad: float32 [1024], replicated
- project_in_grad: float32 [1024, 3, 1024], P(None, None, 'tensor')
- project_out_grad: float32 [1024, 1024], P('tensor')
- second_gain_grad: float32 [1024], replicated
- second_shift_grad: float32 [1024], replicated
- router_grad: float32 [1024, 16], replicated
- mixing_grad: float32 [1024, 2], replicated
- dense_up_grad: float32 [1024, 4096], P(None, 'tensor')
- dense_down_grad: float32 [4096, 1024], P('tensor')
- expert_up_grad: float32 [16, 1024, 4096], P('expert', None, 'tensor')
- expert_down_grad: float32 [16, 4096, 1024], P('expert', 'tensor')
Inputs may be any that keep to these rules, and one draw needn't show every extreme that they name: `routes`: in every block of 1024 tokens (tokens b * 1024 to (b + 1) * 1024 - 1) some expert is named by more than 128 tokens. slot_index[t] is the number of earlier tokens of t's block with the same route, or 128 where that number is 128 or more (the token is dropped); so at most 128 kept tokens of a block name one expert, and every block fills all 128 slots of some expert.
All inputs are finite; a program needn't handle non-finite values.
Results may differ from a plain program's by a relative error of at most 0.023.
Values may be sent and summed in bfloat16 or wider, within the bound.
No kernel may reach another device: no remote copies, remote signals or barrier semaphores. Data moves between devices by JAX's collectives and lax.ppermute only.
A program may use at most 192 MiB of HBM per device.

v0:
```python
import jax
import jax.numpy as jnp
from jax import lax
from jax.sharding import PartitionSpec as P

HEAD_DIM = 64
SEQ = 1024
EPS = 1e-05
NEGATIVE = -1e30


def layer_norm(row_values, norm_gain, norm_shift):
    row_mean = jnp.mean(row_values, axis=-1, keepdims=True)
    centred = row_values - row_mean
    spread = jnp.mean(centred * centred, axis=-1, keepdims=True)
    return centred * lax.rsqrt(spread + EPS) * norm_gain + norm_shift


def gelu_tanh(values):
    return jax.nn.gelu(values, approximate=True)


def gelu_back(pre_act, incoming):
    return jax.vjp(gelu_tanh, pre_act)[1](incoming)[0]


def causal_scores(query_block, key_seq, offset):
    score_scale = HEAD_DIM ** (-0.5)
    scores = (
        jnp.einsum("qhd,khd->hqk", query_block, key_seq, preferred_element_type=jnp.float32)
        * score_scale
    )
    query_pos = offset + lax.iota(jnp.int32, query_block.shape[0])
    key_pos = lax.iota(jnp.int32, key_seq.shape[0])
    allowed = key_pos[None, :] <= query_pos[:, None]
    return jnp.where(allowed[None], scores, NEGATIVE)


def attend_forward(queries, key_rows, values, block_rows):
    row_count, head_count, head_width = queries.shape
    per_seq = SEQ // block_rows

    def one_block(block_index):
        seq_start = block_index // per_seq * SEQ
        offset = block_index % per_seq * block_rows
        query_block = lax.dynamic_slice_in_dim(queries, seq_start + offset, block_rows, 0)
        scores = causal_scores(query_block, key_rows, offset)
        row_max = jnp.max(scores, axis=-1, keepdims=True)
        powers = jnp.exp(scores - row_max)
        row_total = jnp.sum(powers, axis=-1, keepdims=True)
        weights = (powers / row_total).astype(jnp.bfloat16)
        blended = jnp.einsum("hqk,khd->qhd", weights, values, preferred_element_type=jnp.float32)
        return (blended.astype(jnp.bfloat16), (row_max + jnp.log(row_total))[..., 0])

    blended, log_total = lax.map(one_block, jnp.arange(row_count // block_rows, dtype=jnp.int32))
    return (blended.reshape(row_count, head_count * head_width), log_total)


def attend_backward(queries, key_rows, values, log_total, grad_blended, block_rows):
    row_count, head_count, head_width = queries.shape
    per_seq = SEQ // block_rows
    score_scale = HEAD_DIM ** (-0.5)

    def one_seq(sequence):
        seq_start = sequence * SEQ

        def step(totals, inner_index):
            key_acc, value_acc = totals
            offset = inner_index * block_rows
            query_block = lax.dynamic_slice_in_dim(queries, seq_start + offset, block_rows, 0)
            grad_block = lax.dynamic_slice_in_dim(grad_blended, seq_start + offset, block_rows, 0)
            row_log = lax.dynamic_index_in_dim(
                log_total, sequence * per_seq + inner_index, 0, keepdims=False
            )
            scores = causal_scores(query_block, key_rows, offset)
            weights = jnp.exp(scores - row_log[..., None])
            weight_grad = jnp.einsum(
                "qhd,khd->hqk", grad_block, values, preferred_element_type=jnp.float32
            )
            row_inner = jnp.sum(weights * weight_grad, axis=-1, keepdims=True)
            score_grad = (weights * (weight_grad - row_inner)).astype(jnp.bfloat16)
            query_grad = (
                jnp.einsum("hqk,khd->qhd", score_grad, key_rows, preferred_element_type=jnp.float32)
                * score_scale
            )
            key_acc = (
                key_acc
                + jnp.einsum(
                    "hqk,qhd->khd", score_grad, query_block, preferred_element_type=jnp.float32
                )
                * score_scale
            )
            value_acc = value_acc + jnp.einsum(
                "hqk,qhd->khd",
                weights.astype(jnp.bfloat16),
                grad_block,
                preferred_element_type=jnp.float32,
            )
            return ((key_acc, value_acc), query_grad)

        empty_acc = jnp.zeros((SEQ, head_count, head_width), jnp.float32)
        (key_grad, value_grad), query_grad = lax.scan(
            step, (empty_acc, empty_acc), jnp.arange(per_seq, dtype=jnp.int32)
        )
        return (query_grad.reshape(SEQ, head_count, head_width), key_grad, value_grad)

    query_grad, key_grad, value_grad = lax.map(
        one_seq, jnp.arange(row_count // SEQ, dtype=jnp.int32)
    )
    flat_width = head_count * head_width
    return jnp.stack(
        [
            query_grad.reshape(row_count, flat_width),
            key_grad.reshape(row_count, flat_width),
            value_grad.reshape(row_count, flat_width),
        ],
        axis=1,
    )


def send_home(buffer):
    return lax.all_to_all(
        buffer.astype(jnp.bfloat16), "expert", split_axis=1, concat_axis=0, tiled=True
    ).astype(buffer.dtype)


def send_grads_home(buffer):
    return lax.all_to_all(
        buffer.astype(jnp.bfloat16), "expert", split_axis=1, concat_axis=0, tiled=True
    ).astype(buffer.dtype)


def local(
    tokens,
    cotangent,
    routes,
    slot_index,
    first_gain,
    first_shift,
    project_in,
    project_out,
    second_gain,
    second_shift,
    router_weight,
    mixing_weight,
    dense_up,
    dense_down,
    expert_up,
    expert_down,
):
    inputs = tokens.astype(jnp.float32)
    cotan_rows = cotangent.astype(jnp.float32)
    row_count, model_width = inputs.shape
    expert_count = router_weight.shape[1]
    capacity = 2 * row_count // expert_count
    head_count = project_in.shape[2] // HEAD_DIM
    block_rows = min(512, SEQ)
    normed_in, first_back = jax.vjp(layer_norm, inputs, first_gain, first_shift)
    normed_low = normed_in.astype(jnp.bfloat16)
    projected = jnp.einsum(
        "td,dcn->tcn", normed_low, project_in, preferred_element_type=jnp.float32
    ).astype(jnp.bfloat16)
    queries = projected[:, 0].reshape(row_count, head_count, HEAD_DIM)
    key_rows = projected[:, 1].reshape(row_count, head_count, HEAD_DIM)
    values = projected[:, 2].reshape(row_count, head_count, HEAD_DIM)
    attended, log_total = attend_forward(queries, key_rows, values, block_rows)
    attn_part = jnp.dot(attended, project_out, preferred_element_type=jnp.float32)
    attn_full = lax.psum(attn_part, "tensor")
    residual = inputs + attn_full
    normed_mid, second_back = jax.vjp(layer_norm, residual, second_gain, second_shift)
    mid_low = normed_mid.astype(jnp.bfloat16)
    router_logits = jnp.dot(mid_low, router_weight, preferred_element_type=jnp.float32)
    mixing_logits = jnp.dot(mid_low, mixing_weight, preferred_element_type=jnp.float32)
    chosen = routes[:, None] == lax.iota(jnp.int32, expert_count)[None, :]

    def gating(route_logits, mix_logits):
        router_probs = jax.nn.softmax(route_logits, axis=-1)
        return (
            jnp.sum(jnp.where(chosen, router_probs, 0.0), axis=-1),
            jax.nn.softmax(mix_logits, axis=-1),
        )

    (gate_value, mixing), gating_back = jax.vjp(gating, router_logits, mixing_logits)
    slot_total = expert_count * capacity
    slot_place = jnp.where(slot_index < capacity, routes * capacity + slot_index, slot_total)
    holder = (
        jnp.full((slot_total,), row_count, jnp.int32)
        .at[slot_place]
        .set(lax.iota(jnp.int32, row_count), mode="drop")
    )

    def to_slots(row_values):
        taken = jnp.take(row_values, holder, axis=0, mode="fill", fill_value=0)
        return taken.reshape(expert_count, capacity, row_values.shape[1])

    def from_slots(buffer):
        return jnp.take(
            buffer.reshape(slot_total, buffer.shape[-1]),
            slot_place,
            axis=0,
            mode="fill",
            fill_value=0,
        )

    arrived = lax.all_to_all(to_slots(mid_low), "expert", split_axis=0, concat_axis=1, tiled=True)
    expert_pre = jnp.einsum("erd,edf->erf", arrived, expert_up, preferred_element_type=jnp.float32)
    expert_hidden = gelu_tanh(expert_pre).astype(jnp.bfloat16)
    expert_part = jnp.einsum(
        "erf,efd->erd", expert_hidden, expert_down, preferred_element_type=jnp.float32
    )
    dense_pre = jnp.dot(mid_low, dense_up, preferred_element_type=jnp.float32)
    dense_hidden = gelu_tanh(dense_pre).astype(jnp.bfloat16)
    dense_part = jnp.dot(dense_hidden, dense_down, preferred_element_type=jnp.float32)
    dense_weight = mixing[:, 0:1]
    expert_weight = (mixing[:, 1] * gate_value)[:, None]
    dense_full, expert_full = (
        lax.psum(dense_part.astype(jnp.bfloat16), "tensor").astype(jnp.float32),
        lax.psum(expert_part.astype(jnp.bfloat16), "tensor").astype(jnp.float32),
    )
    expert_tok = from_slots(send_home(expert_full))
    layer_out = residual + dense_weight * dense_full + expert_weight * expert_tok
    dense_dot = jnp.sum(cotan_rows * dense_full, axis=-1)
    expert_dot = jnp.sum(cotan_rows * expert_tok, axis=-1)
    dense_out_grad = (cotan_rows * dense_weight).astype(jnp.bfloat16)
    expert_tok_grad = (cotan_rows * expert_weight).astype(jnp.bfloat16)
    mixing_dots = jnp.stack([dense_dot, gate_value * expert_dot], axis=-1)
    gate_grad = mixing[:, 1] * expert_dot
    router_logit_grad, mixing_logit_grad = gating_back((gate_grad, mixing_dots))
    router_low = router_logit_grad.astype(jnp.bfloat16)
    mixing_low = mixing_logit_grad.astype(jnp.bfloat16)
    router_grad = jnp.einsum("td,te->de", mid_low, router_low, preferred_element_type=jnp.float32)
    mixing_grad = jnp.einsum("td,te->de", mid_low, mixing_low, preferred_element_type=jnp.float32)
    mid_from_gates = jnp.einsum(
        "te,de->td", router_low, router_weight, preferred_element_type=jnp.float32
    ) + jnp.einsum("te,de->td", mixing_low, mixing_weight, preferred_element_type=jnp.float32)
    dense_down_grad = jnp.einsum(
        "tf,td->fd", dense_hidden, dense_out_grad, preferred_element_type=jnp.float32
    )
    dense_hidden_grad = jnp.einsum(
        "td,fd->tf", dense_out_grad, dense_down, preferred_element_type=jnp.float32
    )
    dense_pre_grad = gelu_back(dense_pre, dense_hidden_grad).astype(jnp.bfloat16)
    dense_up_grad = jnp.einsum(
        "td,tf->df", mid_low, dense_pre_grad, preferred_element_type=jnp.float32
    )
    mid_dense_part = jnp.einsum(
        "tf,df->td", dense_pre_grad, dense_up, preferred_element_type=jnp.float32
    )
    grad_arrived = lax.all_to_all(
        to_slots(expert_tok_grad), "expert", split_axis=0, concat_axis=1, tiled=True
    )
    expert_down_grad = jnp.einsum(
        "erf,erd->efd", expert_hidden, grad_arrived, preferred_element_type=jnp.float32
    )
    expert_hidden_grad = jnp.einsum(
        "erd,efd->erf", grad_arrived, expert_down, preferred_element_type=jnp.float32
    )
    expert_pre_grad = gelu_back(expert_pre, expert_hidden_grad).astype(jnp.bfloat16)
    expert_up_grad = jnp.einsum(
        "erd,erf->edf", arrived, expert_pre_grad, preferred_element_type=jnp.float32
    )
    arrived_grad = jnp.einsum(
        "erf,edf->erd", expert_pre_grad, expert_up, preferred_element_type=jnp.float32
    )
    mid_dense, arrived_full = (
        lax.psum(mid_dense_part.astype(jnp.bfloat16), "tensor").astype(jnp.float32),
        lax.psum(arrived_grad.astype(jnp.bfloat16), "tensor").astype(jnp.float32),
    )
    mid_grad = mid_dense + from_slots(send_grads_home(arrived_full)) + mid_from_gates
    resid_from_mid, second_gain_grad, second_shift_grad = second_back(mid_grad)
    residual_grad = cotan_rows + resid_from_mid
    attn_grad_low = residual_grad.astype(jnp.bfloat16)
    project_out_grad = jnp.einsum(
        "tn,td->nd", attended, attn_grad_low, preferred_element_type=jnp.float32
    )
    attended_grad = jnp.einsum(
        "td,nd->tn", attn_grad_low, project_out, preferred_element_type=jnp.float32
    ).astype(jnp.bfloat16)
    qkv_grad = attend_backward(
        queries,
        key_rows,
        values,
        log_total,
        attended_grad.reshape(row_count, head_count, HEAD_DIM),
        block_rows,
    ).astype(jnp.bfloat16)
    project_in_grad = jnp.einsum(
        "td,tcn->dcn", normed_low, qkv_grad, preferred_element_type=jnp.float32
    )
    normed_part = jnp.einsum(
        "tcn,dcn->td", qkv_grad, project_in, preferred_element_type=jnp.float32
    )
    normed_grad = lax.psum(normed_part.astype(jnp.bfloat16), "tensor").astype(jnp.float32)
    input_from_norm, first_gain_grad, first_shift_grad = first_back(normed_grad)
    input_grad = (residual_grad + input_from_norm).astype(jnp.bfloat16)
    (
        router_grad,
        mixing_grad,
        dense_up_grad,
        dense_down_grad,
        second_gain_grad,
        second_shift_grad,
        project_out_grad,
        project_in_grad,
        first_gain_grad,
        first_shift_grad,
    ) = (
        lax.psum(router_grad.astype(jnp.bfloat16), "expert").astype(jnp.float32),
        lax.psum(mixing_grad.astype(jnp.bfloat16), "expert").astype(jnp.float32),
        lax.psum(dense_up_grad.astype(jnp.bfloat16), "expert").astype(jnp.float32),
        lax.psum(dense_down_grad.astype(jnp.bfloat16), "expert").astype(jnp.float32),
        lax.psum(second_gain_grad.astype(jnp.bfloat16), "expert").astype(jnp.float32),
        lax.psum(second_shift_grad.astype(jnp.bfloat16), "expert").astype(jnp.float32),
        lax.psum(project_out_grad.astype(jnp.bfloat16), "expert").astype(jnp.float32),
        lax.psum(project_in_grad.astype(jnp.bfloat16), "expert").astype(jnp.float32),
        lax.psum(first_gain_grad.astype(jnp.bfloat16), "expert").astype(jnp.float32),
        lax.psum(first_shift_grad.astype(jnp.bfloat16), "expert").astype(jnp.float32),
    )
    return (
        layer_out.astype(jnp.bfloat16),
        input_grad,
        first_gain_grad,
        first_shift_grad,
        project_in_grad,
        project_out_grad,
        second_gain_grad,
        second_shift_grad,
        router_grad,
        mixing_grad,
        dense_up_grad,
        dense_down_grad,
        expert_up_grad,
        expert_down_grad,
    )


def solution(mesh):
    placed = (
        P("expert", None),
        P("expert", None),
        P("expert"),
        P("expert"),
        P(),
        P(),
        P(None, None, "tensor"),
        P("tensor", None),
        P(),
        P(),
        P(),
        P(),
        P(None, "tensor"),
        P("tensor", None),
        P("expert", None, "tensor"),
        P("expert", "tensor", None),
    )
    return jax.shard_map(
        local,
        mesh=mesh,
        in_specs=placed,
        out_specs=(
            P("expert", None),
            P("expert", None),
            P(),
            P(),
            P(None, None, "tensor"),
            P("tensor", None),
            P(),
            P(),
            P(),
            P(),
            P(None, "tensor"),
            P("tensor", None),
            P("expert", None, "tensor"),
            P("expert", "tensor", None),
        ),
        check_vma=False,
    )
```

profile of v0, /device:TPU:0, one launch (start us, length us, event | category | flops | bytes accessed | tf_op | source)
XLA Modules:
  0.0 1272.1 jit_solution(15387023293925295045)
XLA Ops:
  16.1 23.0 %while.43 = (s32[]{:T(128)}, bf16[2,512,4,64]{1,3,2,0:T(8,128)(2,1)}, f32[2,4,512]{2,1,0:T(4,128)S(1)}, s32[2]{0:T(128)S(1)}, bf16[1024,4,64]{0,2,1:T(8,128)(2,1...) while((s32[]{:T(128)}, ...), condition=%wide.region_5.6_spmd, body=%wide.region_2.5_spmd.sunk | while | flops 562690560 | bytes 35197428 | solution.py:55
  41.9 3.8 fusion.104
  46.4 4.5 scatter_custom_fusion
  50.9 152.7 %all-reduce.10.cloned.1.call-done = f32[1024,1024]{1,0:T(8,128)} async-done(((f32[1024,1024]{1,0:T(8,128)}), f32[1024,1024]{1,0:T(8,128)}) %all-reduce.10.cloned.1.call-update) | async-done | bytes 4194320 | tf_op jit(solution)/shard_map/psum | solution.py:168
  203.6 3.3 fusion.99
  211.6 12.8 %gather_fusion = bf16[2048,1024]{1,0:T(8,128)(2,1)} fusion(bf16[1024,1024]{1,0:T(8,128)(2,1)} %add_convert_fusion.1, s32[2048]{0:T(1024)S(1)} %fusion.86), kind=kCustom, calls=%fused_computation.clone | custom fusion | bytes 8396800 | tf_op jit(solution)/shard_map/jit(_take)/gather | solution.py:193
  224.4 3.8 broadcast_select_fusion.1
  228.2 4.6 all-to-all-start
  232.8 4.6 fusion.105
  239.4 4.0 convolution_convert_fusion.5
  243.4 38.5 %all-to-all-done = bf16[16,128,1024]{2,1,0:T(8,128)(2,1)} async-done(((bf16[16,128,1024]{2,1,0:T(8,128)(2,1)}), bf16[16,128,1024]{2,1,0:T(8,128)(2,1)}, u32[]{:S(2)}, u32[]{:S(2)}) %all-to-all-start) | async-done | bytes 4194336 | tf_op jit(solution)/shard_map/all_to_all | solution.py:205
  286.7 4.5 fusion.106
  291.2 3.4 copy-done.81
  294.6 6.8 convolution_convert_fusion.1
  301.4 220.2 %all-reduce.18.cloned.1.call-done = (bf16[1024,1024]{1,0:T(8,128)(2,1)}, bf16[2,1024,1024]{2,1,0:T(8,128)(2,1)}) async-done(((bf16[1024,1024]{1,0:T(8,128)(2,1)}, bf16[2,1024,1024]{2,1,0:T(8,128)(2,1)}), (bf16[1024,1024]{1,0:T(8,128)(2,1)}, bf16[2,1024,1024]{2,1,0:T(8,128)(2,1)})) %all-reduce.18.cloned.1.call-update) | async-done | bytes 6291472 | tf_op jit(solution)/shard_map/psum | solution.py:217
  521.6 8.5 copy.55
  530.2 4.7 all-to-all-start.1
  539.6 44.4 %all-to-all-done.1 = bf16[2,1024,1024]{2,0,1:T(2,128)(2,1)} async-done(((bf16[2,1024,1024]{2,0,1:T(2,128)(2,1)}), bf16[2,1024,1024]{2,0,1:T(2,128)(2,1)}, u32[]{:S(2)}, u32[]{:S(2)}) %all-to-all-start.1) | async-done | bytes 4194336 | tf_op jit(solution)/shard_map/all_to_all | solution.py:122
  584.0 7.1 copy.56
  591.1 9.7 gather_fusion.1
  600.8 4.5 fusion.68
  607.2 12.8 %gather_fusion.2 = bf16[2048,1024]{1,0:T(8,128)(2,1)} fusion(bf16[1024,1024]{1,0:T(8,128)(2,1)} %fusion.66, s32[2048]{0:T(1024)S(1)} %fusion.86), kind=kCustom, calls=%fused_computation.2.clone | custom fusion | bytes 8396800 | tf_op jit(solution)/shard_map/jit(_take)/gather | solution.py:193
  620.0 3.8 broadcast_select_fusion
  623.8 4.6 all-to-all-start.2
  628.5 7.7 fusion.62
  637.6 3.7 convolution_convert_fusion.4
  641.3 36.3 %all-to-all-done.2 = bf16[16,128,1024]{2,1,0:T(8,128)(2,1)} async-done(((bf16[16,128,1024]{2,1,0:T(8,128)(2,1)}), bf16[16,128,1024]{2,1,0:T(8,128)(2,1)}, u32[]{:S(2)}, u32[]{:S(2)}) %all-to-all-start.2) | async-done | bytes 4194336 | tf_op jit(solution)/shard_map/all_to_all | solution.py:249
  681.0 12.1 fusion.43
  695.1 6.2 convolution_convert_fusion
  701.3 220.1 %all-reduce.16.cloned.1.call-done = (bf16[2,1024,1024]{2,1,0:T(8,128)(2,1)}, bf16[1024,1024]{1,0:T(8,128)(2,1)}) async-done(((bf16[2,1024,1024]{2,1,0:T(8,128)(2,1)}, bf16[1024,1024]{1,0:T(8,128)(2,1)}), (bf16[2,1024,1024]{2,1,0:T(8,128)(2,1)}, bf16[1024,1024]{1,0:T(8,128)(2,1)})) %all-reduce.16.cloned.1.call-update) | async-done | bytes 6291472 | tf_op jit(solution)/shard_map/psum | solution.py:267
  921.5 8.5 copy.58
  930.0 4.7 all-to-all-start.3
  939.6 44.2 %all-to-all-done.3 = bf16[2,1024,1024]{2,0,1:T(2,128)(2,1)} async-done(((bf16[2,1024,1024]{2,0,1:T(2,128)(2,1)}), bf16[2,1024,1024]{2,0,1:T(2,128)(2,1)}, u32[]{:S(2)}, u32[]{:S(2)}) %all-to-all-start.3) | async-done | bytes 4194336 | tf_op jit(solution)/shard_map/all_to_all | solution.py:128
  983.8 7.1 copy.59
  990.9 9.8 gather_fusion.3
  1000.8 7.5 multiply_reduce_fusion.1
  1009.0 3.6 fusion.98
  1016.7 33.2 %while.44 = (s32[]{:T(128)}, f32[1024,4,64]{0,2,1:T(8,128)}, f32[1024,4,64]{0,2,1:T(8,128)}, bf16[2,512,4,64]{1,3,2,0:T(8,128)(2,1)}, s32[2]{0:T(128)S(1)}, /*in...) while((s32[]{:T(128)}, f32[1024,4,64]{0,2,1:T(8,128)}, ...), condition=%wide.region_27.30_spmd.clone, body=%wide.region_25.29_spmd.clone.sunk | while | flops 1375599104 | bytes 97579512 | solution.py:102
  1057.6 4.9 bitcast_convert_fusion
  1063.0 5.5 convolution_convert_fusion.3
  1068.5 4.4 convolution_convert_fusion.2
  1077.9 13.6 %fusion.97 = f32[2,1024,1024]{2,1,0:T(8,128)} fusion(bf16[2,1024,1024]{2,1,0:T(8,128)(2,1)} %bitcast.152, f32[2,1024,1024]{2,1,0:T(8,128)} %copy-done.81), kind=kOutput, calls=%fused_computation.170 | convolution fusion | flops 4313841664 | bytes 20971520 | tf_op jit(solution)/shard_map/erf,erd->efd/dot_general | solution.py:252
  1091.5 6.9 fusion.107
  1098.4 47.4 %all-reduce.12.cloned.1.call-done = bf16[1024,1024]{1,0:T(8,128)(2,1)} async-done(((bf16[1024,1024]{1,0:T(8,128)(2,1)}), bf16[1024,1024]{1,0:T(8,128)(2,1)}) %all-reduce.12.cloned.1.call-update) | async-done | bytes 2097168 | tf_op jit(solution)/shard_map/psum | solution.py:293
  1153.4 26.6 %all-reduce = (bf16[1024]{0:T(1024)(128)(2,1)S(1)}, bf16[1024]{0:T(1024)(128)(2,1)S(1)}, bf16[1024]{0:T(1024)(128)(2,1)S(1)}, bf16[1024]{0:T(1024)(128)(2,1)S(1)...) all-reduce(bf16[1024]{0:T(1024)(128)(2,1)S(1)} %get-tuple-element.3, ...), channel_id=1, replica_groups=mesh['expert'=8,'tensor'=4] {'expert'}, use_global_device_ids=true, to_apply=%region_32.35 | all-reduce | flops 22528 | bytes 90112 | tf_op jit(solution)/shard_map/psum | solution.py:316
  1183.6 5.5 add_convert_fusion
  1189.1 65.5 %all-reduce.14.cloned.1.call-done = (bf16[1024,3,256]{2,0,1:T(8,128)(2,1)}, bf16[256,1024]{1,0:T(8,128)(2,1)}, bf16[1024,1024]{1,0:T(8,128)(2,1)}, bf16[1024,1024]{1,0:T(8,128)(2,1)}) async-done(((bf16[1024,3,256]{2,0,1:T(8,128)(2,1)}, bf16[256,1024]{1,0:T(8,128)(2,1)}, bf16[1024,1024]{1,0:T(8,128)(2,1)}, bf16[1024,1024]{1,0:T(8,128)(2,1)}), (bf16[1024,3,256]{2,0,1:T(8,128)(2,1)}, ...) | async-done | bytes 6291472 | tf_op jit(solution)/shard_map/psum | solution.py:315
  1256.9 3.3 convert_element_type.230
  (305 shorter events, 123.2 us)
Async XLA Ops:
  7.2 232.2 %copy-start = (bf16[1024,1024]{1,0:T(8,128)(2,1)S(1)}, bf16[1024,1024]{1,0:T(8,128)(2,1)}, u32[]{:S(2)}) copy-start(bf16[1024,1024]{1,0:T(8,128)(2,1)} %param.37) | copy-start | bytes 6291460
  7.2 5.8 copy-start.55
  7.2 5.7 copy-start.77
  7.2 196.4 %all-reduce.10.cloned.1.call-start = ((), (), s32[]{:S(2)}) async-start(), calls=%async_computation.4 | async-start | bytes 8388608 | tf_op jit(solution)/shard_map/psum | solution.py:168
  7.3 5.7 copy-start.9
  7.3 5.7 copy-start.76
  9.4 5.8 copy-start.44
  39.0 6.6 copy-start.3
  39.0 6.6 copy-start.11
  39.1 6.6 copy-start.46
  207.6 16.8 %copy-start.63 = (f32[1024]{0:T(1024)}, f32[1024]{0:T(1024)S(1)}, u32[]{:S(2)}) copy-start(f32[1024]{0:T(1024)S(1)} %multiply_reduce_fusion.3) | copy-start | bytes 12292
  228.2 53.7 %all-to-all-start = ((bf16[16,128,1024]{2,1,0:T(8,128)(2,1)}), bf16[16,128,1024]{2,1,0:T(8,128)(2,1)}, u32[]{:S(2)}, u32[]{:S(2)}) async-start(bf16[16,128,1024]{2,1,0:T(8,128)(2,1)} %bitcast.148), calls=%async_computation | async-start | bytes 8388608 | tf_op jit(solution)/shard_map/all_to_all | solution.py:205
  232.8 288.9 %all-reduce.18.cloned.1.call-start = ((), (), s32[]{:S(2)}) async-start(), calls=%async_computation.8 | async-start | bytes 12582912 | tf_op jit(solution)/shard_map/psum | solution.py:217
  286.7 7.9 copy-start.71
  530.2 7.1 copy-start.42
  530.2 53.8 %all-to-all-start.1 = ((bf16[2,1024,1024]{2,0,1:T(2,128)(2,1)}), bf16[2,1024,1024]{2,0,1:T(2,128)(2,1)}, u32[]{:S(2)}, u32[]{:S(2)}) async-start(bf16[2,1024,1024]{2,0,1:T(2,128)(2,1)} %copy.55), calls=%async_computation.1 | async-start | bytes 8388608 | tf_op jit(solution)/shard_map/all_to_all | solution.py:122
  623.8 53.7 %all-to-all-start.2 = ((bf16[16,128,1024]{2,1,0:T(8,128)(2,1)}), bf16[16,128,1024]{2,1,0:T(8,128)(2,1)}, u32[]{:S(2)}, u32[]{:S(2)}) async-start(bf16[16,128,1024]{2,1,0:T(8,128)(2,1)} %bitcast.147), calls=%async_computation.2 | async-start | bytes 8388608 | tf_op jit(solution)/shard_map/all_to_all | solution.py:249
  628.4 293.0 %all-reduce.16.cloned.1.call-start = ((), (), s32[]{:S(2)}) async-start(), calls=%async_computation.7 | async-start | bytes 12582912 | tf_op jit(solution)/shard_map/psum | solution.py:267
  628.5 9.1 copy-start.75
  680.4 12.7 copy-start.24
  681.0 14.1 %copy-start.74 = (bf16[2,1024,1024]{2,1,0:T(8,128)(2,1)S(1)}, bf16[2,1024,1024]{2,1,0:T(8,128)(2,1)}, u32[]{:S(2)}) copy-start(bf16[2,1024,1024]{2,1,0:T(8,128)(2,1)} %param.38) | copy-start | bytes 12582916
  930.0 53.8 %all-to-all-start.3 = ((bf16[2,1024,1024]{2,0,1:T(2,128)(2,1)}), bf16[2,1024,1024]{2,0,1:T(2,128)(2,1)}, u32[]{:S(2)}, u32[]{:S(2)}) async-start(bf16[2,1024,1024]{2,0,1:T(2,128)(2,1)} %copy.58), calls=%async_computation.3 | async-start | bytes 8388608 | tf_op jit(solution)/shard_map/all_to_all | solution.py:128
  934.7 211.2 %all-reduce.12.cloned.1.call-start = ((), (), s32[]{:S(2)}) async-start(), calls=%async_computation.5 | async-start | bytes 4194304 | tf_op jit(solution)/shard_map/psum | solution.py:293
  990.9 9.8 copy-start.49
  990.9 9.8 copy-start.51
  990.9 9.8 copy-start.54
  1000.7 7.6 copy-start.64
  1000.7 7.6 copy-start.6
  1000.7 7.7 copy-start.13
  1000.7 8.3 copy-start.21
  1062.5 192.2 %all-reduce.14.cloned.1.call-start = ((), (), s32[]{:S(2)}) async-start(), calls=%async_computation.6 | async-start | bytes 12582912 | tf_op jit(solution)/shard_map/psum | solution.py:315
  1062.9 5.5 copy-start.17
  1068.4 6.0 copy-start.10
  1068.4 6.0 copy-start.38
  1068.4 6.0 copy-start.39
  1068.5 6.0 copy-start.45
  1068.5 6.0 copy-start.56
  1068.5 6.0 copy-start.58
  1068.5 6.0 copy-start.78
  1077.8 13.7 %copy-start.23 = (bf16[2,8,128,1024]{3,2,1,0:T(8,128)(2,1)S(1)}, bf16[2,8,128,1024]{3,2,1,0:T(8,128)(2,1)}, u32[]{:S(2)}) copy-start(bf16[2,8,128,1024]{3,2,1,0:T(8,128)(2,1)} %copy-done.22) | copy-start | bytes 12582916
  1077.9 13.6 %copy-start.83 = (bf16[2,1024,1024]{2,1,0:T(8,128)(2,1)S(1)}, bf16[2,1024,1024]{2,1,0:T(8,128)(2,1)}, u32[]{:S(2)}) copy-start(bf16[2,1024,1024]{2,1,0:T(8,128)(2,1)} %copy-done.82) | copy-start | bytes 12582916
  1098.4 52.2 %copy-start.62 = (f32[1024]{0:T(1024)S(1)}, f32[1024]{0:T(1024)}, u32[]{:S(2)}) copy-start(f32[1024]{0:T(1024)} %copy-done.61) | copy-start | bytes 12292
  1147.8 5.5 copy-start.43
  1147.9 5.5 copy-start.65
  1147.9 5.5 copy-start.67
  1147.9 5.5 copy-start.68
  1147.9 35.8 %copy-start.60 = (f32[1024]{0:T(1024)S(1)}, f32[1024]{0:T(1024)}, u32[]{:S(2)}) copy-start(f32[1024]{0:T(1024)} %copy-done.59) | copy-start | bytes 12292
  1254.7 5.6 copy-start.29
  (57 other events, 132.2 us)
Sparse Core Ops, SparseCore 0:
  45.9 157.6 all-reduce.9
  301.6 220.0 all-reduce.17
  701.5 219.9 all-reduce.15
  1062.6 83.2 all-reduce.11
  1150.5 104.1 all-reduce.13
where the time goes:
time: 1280 us; the launch traced here: 1270 us
  waiting for transfers between devices  869 us (68%)
  matrix products  142 us (11%)
  local copies, waits for them, and re-layouts  119 us (9%)
  other arithmetic  69.5 us (5%)
  blocking collectives  26.6 us (2%)
  starting transfers between devices  19.2 us (2%)
  between operations  14.9 us (1%)
    psum x1, waiting for transfers between devices, local(): lax.psum(dense_part.astype(jnp.bfloat16), 'tensor').astype(jnp.float32)  220 us
    psum x1, waiting for transfers between devices, local(): lax.psum(arrived_grad.astype(jnp.bfloat16), 'tensor').astype(jnp.float32)  220 us
    psum x1, waiting for transfers between devices, local(): attn_full = lax.psum(attn_part, 'tensor')  153 us
    psum x1, waiting for transfers between devices, local(): lax.psum(project_in_grad.astype(jnp.bfloat16), 'expert').astype(jnp.float32)  65.5 us
    psum x1, waiting for transfers between devices, local(): lax.psum(normed_part.astype(jnp.bfloat16), 'tensor').astype(jnp.float32)  47.4 us
    all_to_all x1, waiting for transfers between devices, send_home(): lax.all_to_all(buffer.astype(jnp.bfloat16), 'expert', split_axis=1, conca...  44.4 us
    all_to_all x1, waiting for transfers between devices, send_grads_home(): lax.all_to_all(buffer.astype(jnp.bfloat16), 'expert', split_axis=1, conca...  44.2 us
    all_to_all x1, waiting for transfers between devices, local(): lax.all_to_all(to_slots(mid_low), 'expert', split_axis=0, concat_axis=1,...  38.5 us
  transfers between devices with their start and end apart: 9, of which 9 were waited for; matrix products, arithmetic and copies ran while one was open for 7% of the time, Pallas kernels for 0%

commit v1 on v0

--- a/solution.py
+++ b/solution.py
@@ -1,3 +1,4 @@
+import functools
 import jax
 import jax.numpy as jnp
 from jax import lax
@@ -7,6 +8,17 @@
 SEQ = 1024
 EPS = 1e-05
 NEGATIVE = -1e30
+
+
+def extend_the_orders(a0, link_axis):
+    side_arr = a0
+    k_all = lax.axis_size(link_axis)
+    for jj in [[(pp, pp ^ b) for pp in range(k_all)] for b in (1, 2, 4, 8, 16) if b < k_all]:
+        side_arr = side_arr + lax.ppermute(side_arr, link_axis, jj)
+    return side_arr
+
+
+lane_enter = functools.partial(extend_the_orders, link_axis="tensor")
 
 
 def layer_norm(row_values, norm_gain, norm_shift):
@@ -165,7 +177,7 @@
     values = projected[:, 2].reshape(row_count, head_count, HEAD_DIM)
     attended, log_total = attend_forward(queries, key_rows, values, block_rows)
     attn_part = jnp.dot(attended, project_out, preferred_element_type=jnp.float32)
-    attn_full = lax.psum(attn_part, "tensor")
+    attn_full = lane_enter(attn_part)
     residual = inputs + attn_full
     normed_mid, second_back = jax.vjp(layer_norm, residual, second_gain, second_shift)
     mid_low = normed_mid.astype(jnp.bfloat16)

time: 1280 us -> 1420 us (1.11)
  waiting for transfers between devices: 869 us -> 970 us
  local copies, waits for them, and re-layouts: 119 us -> 150 us
    ppermute x0 -> x2, waiting for transfers between devices: none -> 266 us  [extend_the_orders(): side_arr = side_arr + lax.ppermute(side_arr, link_axis, jj)]
    psum x1 -> x0, waiting for transfers between devices: 153 us -> none  [local(): attn_full = lax.psum(attn_part, 'tensor')]
    unnamed x149 -> x155, local copies, waits for them, and re-layouts: 18.8 us -> 33.1 us
    gather x2 -> x4, local copies, waits for them, and re-layouts: 19.5 us -> 30.2 us  [from_slots(): jnp.take(buffer.reshape(slot_total, buffer.shape[-1]), slot_place, axis=0...]
  transfers between devices with their start and end apart: 9 -> 10, of which waited for: 9 -> 10; matrix products, arithmetic and copies ran while one was open for 7% -> 7% of each run, Pallas kernels for 0% -> 0%
where the time goes in v1:
time: 1420 us; the launch traced here: 1410 us
  waiting for transfers between devices  970 us (68%)
  local copies, waits for them, and re-layouts  150 us (11%)
  matrix products  144 us (10%)
  other arithmetic  72.8 us (5%)
  blocking collectives  26.6 us (2%)
  starting transfers between devices  24.7 us (2%)
  between operations  15.2 us (1%)
    ppermute x2, waiting for transfers between devices, extend_the_orders(): side_arr = side_arr + lax.ppermute(side_arr, link_axis, jj)  266 us
    psum x1, waiting for transfers between devices, local(): lax.psum(dense_part.astype(jnp.bfloat16), 'tensor').astype(jnp.float32)  222 us
    psum x1, waiting for transfers between devices, local(): lax.psum(arrived_grad.astype(jnp.bfloat16), 'tensor').astype(jnp.float32)  220 us
    psum x1, waiting for transfers between devices, local(): lax.psum(project_in_grad.astype(jnp.bfloat16), 'expert').astype(jnp.float32)  61.1 us
    psum x1, waiting for transfers between devices, local(): lax.psum(normed_part.astype(jnp.bfloat16), 'tensor').astype(jnp.float32)  43.6 us
    all_to_all x1, waiting for transfers between devices, send_home(): lax.all_to_all(buffer.astype(jnp.bfloat16), 'expert', split_axis=1, conca...  41 us
    all_to_all x1, waiting for transfers between devices, send_grads_home(): lax.all_to_all(buffer.astype(jnp.bfloat16), 'expert', split_axis=1, conca...  40.5 us
    all_to_all x1, waiting for transfers between devices, local(): lax.all_to_all(to_slots(mid_low), 'expert', split_axis=0, concat_axis=1,...  38.4 us
  transfers between devices with their start and end apart: 10, of which 10 were waited for; matrix products, arithmetic and copies ran while one was open for 7% of the time, Pallas kernels for 0%

profile of v1, /device:TPU:0, one launch (start us, length us, event | category | flops | bytes accessed | tf_op | source)
XLA Modules:
  0.0 1413.3 jit_solution(18000278929201628739)
XLA Ops:
  7.2 4.1 copy.78
  20.0 23.0 %while.43 = (s32[]{:T(128)}, bf16[2,512,4,64]{1,3,2,0:T(8,128)(2,1)}, f32[2,4,512]{2,1,0:T(4,128)S(1)}, s32[2]{0:T(128)S(1)}, bf16[1024,4,64]{0,2,1:T(8,128)(2,1...) while((s32[]{:T(128)}, ...), condition=%wide.region_5.6_spmd, body=%wide.region_2.5_spmd.sunk | while | flops 562690560 | bytes 35197428 | solution.py:67
  50.1 90.6 %collective-permute-done = f32[1024,1024]{0,1:T(8,128)S(1)} collective-permute-done((f32[1024,1024]{0,1:T(8,128)S(1)}, f32[1024,1024]{0,1:T(8,128)S(1)}, u32[]{:S(2)}, u32[]{:S(2)}) %collective-permute-start) | collective-permute-done | bytes 4194336 | tf_op jit(solution)/shard_map/ppermute | solution.py:17
  146.4 4.5 scatter_custom_fusion
  151.0 175.5 %collective-permute-done.1 = f32[1024,1024]{0,1:T(8,128)} collective-permute-done((f32[1024,1024]{0,1:T(8,128)}, f32[1024,1024]{0,1:T(8,128)}, u32[]{:S(2)}, u32[]{:S(2)}) %collective-permute-start.1) | collective-permute-done | bytes 4194336 | tf_op jit(solution)/shard_map/ppermute | solution.py:17
  326.5 5.7 fusion.99
  340.7 12.8 gather_fusion
  357.3 4.6 all-to-all-start
  362.0 4.7 fusion.105
  368.6 3.9 convolution_convert_fusion.5
  372.6 38.4 %all-to-all-done = bf16[16,128,1024]{2,1,0:T(8,128)(2,1)} async-done(((bf16[16,128,1024]{2,1,0:T(8,128)(2,1)}), bf16[16,128,1024]{2,1,0:T(8,128)(2,1)}, u32[]{:S(2)}, u32[]{:S(2)}) %all-to-all-start) | async-done | bytes 4194336 | tf_op jit(solution)/shard_map/all_to_all | solution.py:217
  415.8 4.5 fusion.106
  423.7 7.0 convolution_convert_fusion.1
  430.8 222.2 %all-reduce.15.cloned.1.call-done = (bf16[1024,1024]{0,1:T(8,128)(2,1)}, bf16[2,1024,1024]{2,1,0:T(8,128)(2,1)}) async-done(((bf16[1024,1024]{0,1:T(8,128)(2,1)}, bf16[2,1024,1024]{2,1,0:T(8,128)(2,1)}), (bf16[1024,1024]{0,1:T(8,128)(2,1)}, bf16[2,1024,1024]{2,1,0:T(8,128)(2,1)})) %all-reduce.15.cloned.1.call-update) | async-done | bytes 6291472 | tf_op jit(solution)/shard_map/psum | solution.py:229
  653.0 8.5 copy.85
  661.5 4.8 all-to-all-start.1
  666.3 3.9 copy.88
  674.3 41.0 %all-to-all-done.1 = bf16[2,1024,1024]{2,0,1:T(2,128)(2,1)} async-done(((bf16[2,1024,1024]{2,0,1:T(2,128)(2,1)}), bf16[2,1024,1024]{2,0,1:T(2,128)(2,1)}, u32[]{:S(2)}, u32[]{:S(2)}) %all-to-all-start.1) | async-done | bytes 4194336 | tf_op jit(solution)/shard_map/all_to_all | solution.py:134
  715.3 7.1 copy.86
  722.5 9.7 gather_fusion.1
  732.2 5.3 copy.87
  737.5 4.8 fusion.68
  748.2 12.8 gather_fusion.2
  764.8 4.6 all-to-all-start.2
  769.5 7.4 fusion.62
  782.0 36.5 %all-to-all-done.2 = bf16[16,128,1024]{2,1,0:T(8,128)(2,1)} async-done(((bf16[16,128,1024]{2,1,0:T(8,128)(2,1)}), bf16[16,128,1024]{2,1,0:T(8,128)(2,1)}, u32[]{:S(2)}, u32[]{:S(2)}) %all-to-all-start.2) | async-done | bytes 4194336 | tf_op jit(solution)/shard_map/all_to_all | solution.py:261
  822.0 12.1 fusion.43
  836.1 6.5 convolution_convert_fusion
  842.6 220.1 %all-reduce.13.cloned.1.call-done = (bf16[2,1024,1024]{2,1,0:T(8,128)(2,1)}, bf16[1024,1024]{0,1:T(8,128)(2,1)}) async-done(((bf16[2,1024,1024]{2,1,0:T(8,128)(2,1)}, bf16[1024,1024]{0,1:T(8,128)(2,1)}), (bf16[2,1024,1024]{2,1,0:T(8,128)(2,1)}, bf16[1024,1024]{0,1:T(8,128)(2,1)})) %all-reduce.13.cloned.1.call-update) | async-done | bytes 6291472 | tf_op jit(solution)/shard_map/psum | solution.py:279
  1062.7 8.5 copy.92
  1071.2 4.6 all-to-all-start.3
  1084.4 40.5 %all-to-all-done.3 = bf16[2,1024,1024]{2,0,1:T(2,128)(2,1)} async-done(((bf16[2,1024,1024]{2,0,1:T(2,128)(2,1)}), bf16[2,1024,1024]{2,0,1:T(2,128)(2,1)}, u32[]{:S(2)}, u32[]{:S(2)}) %all-to-all-start.3) | async-done | bytes 4194336 | tf_op jit(solution)/shard_map/all_to_all | solution.py:140
  1124.9 7.1 copy.93
  1132.0 9.8 gather_fusion.3
  1141.8 5.4 copy.94
  1147.2 7.3 multiply_reduce_fusion.1
  1163.0 31.3 %while.44 = (s32[]{:T(128)}, f32[1024,4,64]{0,2,1:T(8,128)S(1)}, f32[1024,4,64]{0,2,1:T(8,128)}, bf16[2,512,4,64]{1,3,2,0:T(8,128)(2,1)}, s32[2]{0:T(128)S(1)}, ...) while((s32[]{:T(128)}, f32[1024,4,64]{0,2,1:T(8,128)S(1)}, ...), condition=%wide.region_26.29_spmd.clone, body=%wide.region_24.28_spmd.clone.sunk | while | flops 1375599104 | bytes 87093672 | solution.py:114
  1198.8 5.1 bitcast_convert_fusion
  1204.2 5.4 convolution_convert_fusion.3
  1209.7 4.5 convolution_convert_fusion.2
  1219.1 13.7 fusion.97
  1232.8 6.9 fusion.107
  1239.7 3.9 copy.104
  1243.7 43.6 %all-reduce.9.cloned.1.call-done = bf16[1024,1024]{0,1:T(8,128)(2,1)} async-done(((bf16[1024,1024]{0,1:T(8,128)(2,1)}), bf16[1024,1024]{0,1:T(8,128)(2,1)}) %all-reduce.9.cloned.1.call-update) | async-done | bytes 2097168 | tf_op jit(solution)/shard_map/psum | solution.py:305
  1294.6 26.6 %all-reduce = (bf16[1024]{0:T(1024)(128)(2,1)S(1)}, bf16[1024]{0:T(1024)(128)(2,1)S(1)}, bf16[1024]{0:T(1024)(128)(2,1)S(1)}, bf16[1024]{0:T(1024)(128)(2,1)S(1)...) all-reduce(bf16[1024]{0:T(1024)(128)(2,1)S(1)} %get-tuple-element.3, ...), channel_id=1, replica_groups=mesh['expert'=8,'tensor'=4] {'expert'}, use_global_device_ids=true, to_apply=%region_31.34 | all-reduce | flops 22528 | bytes 90112 | tf_op jit(solution)/shard_map/psum | solution.py:328
  1323.6 5.7 add_convert_fusion
  1329.3 4.0 copy.105
  1334.5 61.1 %all-reduce.11.cloned.1.call-done = (bf16[1024,3,256]{2,0,1:T(8,128)(2,1)}, bf16[256,1024]{1,0:T(8,128)(2,1)}, bf16[1024,1024]{1,0:T(8,128)(2,1)}, bf16[1024,1024]{1,0:T(8,128)(2,1)}) async-done(((bf16[1024,3,256]{2,0,1:T(8,128)(2,1)}, bf16[256,1024]{1,0:T(8,128)(2,1)}, bf16[1024,1024]{1,0:T(8,128)(2,1)}, bf16[1024,1024]{1,0:T(8,128)(2,1)}), (bf16[1024,3,256]{2,0,1:T(8,128)(2,1)}, ...) | async-done | bytes 6291472 | tf_op jit(solution)/shard_map/psum | solution.py:327
  (305 shorter events, 159.7 us)
Async XLA Ops:
  7.2 361.5 %copy-start = (bf16[1024,1024]{1,0:T(8,128)(2,1)S(1)}, bf16[1024,1024]{1,0:T(8,128)(2,1)}, u32[]{:S(2)}) copy-start(bf16[1024,1024]{1,0:T(8,128)(2,1)} %param.37) | copy-start | bytes 6291460
  7.2 9.6 copy-start.53
  7.2 9.6 copy-start.75
  11.3 5.5 copy-start.6
  11.3 5.5 copy-start.74
  13.4 5.6 copy-start.42
  47.0 99.4 %copy-start.50 = (s32[1024]{0:T(1024)S(1)}, s32[1024]{0:T(1024)}, u32[]{:S(2)}) copy-start(s32[1024]{0:T(1024)} %param.26) | copy-start | bytes 12292
  47.0 99.4 %copy-start.68 = (s32[1024]{0:T(1024)S(1)}, s32[1024]{0:T(1024)}, u32[]{:S(2)}) copy-start(s32[1024]{0:T(1024)} %param.27) | copy-start | bytes 12292
  47.0 93.7 %collective-permute-start = (f32[1024,1024]{0,1:T(8,128)S(1)}, f32[1024,1024]{0,1:T(8,128)S(1)}, u32[]{:S(2)}, u32[]{:S(2)}) collective-permute-start(f32[1024,1024]{0,1:T(8,128)S(1)} %fusion.104), channel_id=1, source_target_pairs={{0,1},{1,0},{2,3},{3,2},{4,5},{5,4},{6,7},{7,6},{8,9},{9,8},{10,11... | collective-permute-start | bytes 12582920 | tf_op jit(solution)/shard_map/ppermute | solution.py:17
  143.6 182.8 %collective-permute-start.1 = (f32[1024,1024]{0,1:T(8,128)}, f32[1024,1024]{0,1:T(8,128)}, u32[]{:S(2)}, u32[]{:S(2)}) collective-permute-start(f32[1024,1024]{0,1:T(8,128)} %add.258), channel_id=1, source_target_pairs={{0,2},{1,3},{2,0},{3,1},{4,6},{5,7},{6,4},{7,5},{8,10},{9,11},{10,... | collective-permute-start | bytes 12582920 | tf_op jit(solution)/shard_map/ppermute | solution.py:17
  332.7 8.0 copy-start.61
  357.3 53.7 %all-to-all-start = ((bf16[16,128,1024]{2,1,0:T(8,128)(2,1)}), bf16[16,128,1024]{2,1,0:T(8,128)(2,1)}, u32[]{:S(2)}, u32[]{:S(2)}) async-start(bf16[16,128,1024]{2,1,0:T(8,128)(2,1)} %bitcast.148), calls=%async_computation | async-start | bytes 8388608 | tf_op jit(solution)/shard_map/all_to_all | solution.py:217
  361.9 291.0 %all-reduce.15.cloned.1.call-start = ((), (), s32[]{:S(2)}) async-start(), calls=%async_computation.7 | async-start | bytes 12582912 | tf_op jit(solution)/shard_map/psum | solution.py:229
  415.8 7.9 copy-start.69
  661.5 53.9 %all-to-all-start.1 = ((bf16[2,1024,1024]{2,0,1:T(2,128)(2,1)}), bf16[2,1024,1024]{2,0,1:T(2,128)(2,1)}, u32[]{:S(2)}, u32[]{:S(2)}) async-start(bf16[2,1024,1024]{2,0,1:T(2,128)(2,1)} %copy.85), calls=%async_computation.1 | async-start | bytes 8388608 | tf_op jit(solution)/shard_map/all_to_all | solution.py:134
  666.2 6.0 copy-start.40
  764.8 53.7 %all-to-all-start.2 = ((bf16[16,128,1024]{2,1,0:T(8,128)(2,1)}), bf16[16,128,1024]{2,1,0:T(8,128)(2,1)}, u32[]{:S(2)}, u32[]{:S(2)}) async-start(bf16[16,128,1024]{2,1,0:T(8,128)(2,1)} %bitcast.147), calls=%async_computation.2 | async-start | bytes 8388608 | tf_op jit(solution)/shard_map/all_to_all | solution.py:261
  769.4 293.3 %all-reduce.13.cloned.1.call-start = ((), (), s32[]{:S(2)}) async-start(), calls=%async_computation.6 | async-start | bytes 12582912 | tf_op jit(solution)/shard_map/psum | solution.py:279
  769.5 8.8 copy-start.73
  821.4 12.7 copy-start.22
  822.0 14.1 copy-start.72
  1071.2 53.7 %all-to-all-start.3 = ((bf16[2,1024,1024]{2,0,1:T(2,128)(2,1)}), bf16[2,1024,1024]{2,0,1:T(2,128)(2,1)}, u32[]{:S(2)}, u32[]{:S(2)}) async-start(bf16[2,1024,1024]{2,0,1:T(2,128)(2,1)} %copy.92), calls=%async_computation.3 | async-start | bytes 8388608 | tf_op jit(solution)/shard_map/all_to_all | solution.py:140
  1075.8 211.5 %all-reduce.9.cloned.1.call-start = ((), (), s32[]{:S(2)}) async-start(), calls=%async_computation.4 | async-start | bytes 4194304 | tf_op jit(solution)/shard_map/psum | solution.py:305
  1141.8 5.4 copy-start.47
  1141.8 5.4 copy-start.49
  1141.8 5.4 copy-start.52
  1147.2 7.3 copy-start.62
  1147.2 7.3 copy-start.5
  1147.2 7.7 copy-start.15
  1147.2 8.3 copy-start.19
  1198.8 5.4 copy-start.8
  1203.9 191.8 %all-reduce.11.cloned.1.call-start = ((), (), s32[]{:S(2)}) async-start(), calls=%async_computation.5 | async-start | bytes 12582912 | tf_op jit(solution)/shard_map/psum | solution.py:327
  1204.2 5.4 copy-start.11
  1204.2 5.4 copy-start.78
  1209.6 6.1 copy-start.7
  1209.6 6.1 copy-start.36
  1209.6 6.1 copy-start.37
  1209.6 6.1 copy-start.43
  1209.7 6.1 copy-start.54
  1209.7 6.1 copy-start.56
  1209.7 6.1 copy-start.76
  1219.0 13.8 copy-start.21
  1219.0 13.8 copy-start.82
  1243.7 48.2 %copy-start.60 = (f32[1024]{0:T(1024)S(1)}, f32[1024]{0:T(1024)}, u32[]{:S(2)}) copy-start(f32[1024]{0:T(1024)} %copy-done.59) | copy-start | bytes 12292
  1289.3 5.3 copy-start.41
  1289.3 5.3 copy-start.64
  1289.3 34.3 %copy-start.58 = (f32[1024]{0:T(1024)S(1)}, f32[1024]{0:T(1024)}, u32[]{:S(2)}) copy-start(f32[1024]{0:T(1024)} %copy-done.57) | copy-start | bytes 12292
  1395.7 5.6 copy-start.27
  (53 other events, 143.4 us)
Sparse Core Ops, SparseCore 0:
  430.9 222.0 all-reduce.14
  842.7 219.9 all-reduce.12
  1204.0 83.2 all-reduce.8
  1291.3 104.2 all-reduce.10
